TPU v7x, 32 devices: a whole 2x2x4 slice. The times are simulated.
32 devices in a mesh: dp: 8 (over y, x, core), fsdp: 4 (over z).
Axes of the slice: x: 2, y: 2, z: 4, core: 2. Of those that a mesh axis runs over, the one named last changes fastest.
Arguments:
- tokens: bfloat16 [64, 1024, 768], P('dp', 'fsdp'), may hold values from -6 to 6
- cotangent: bfloat16 [64, 1024, 768], P('dp', 'fsdp'), may hold values from -6 to 6
- lengths: int32 [8, 8], P('dp'), may hold values from 256 to 1024, as said below
- perm: int32 [8, 8], P('dp'), may hold values from 0 to 7, each once within a row
- ln1_gain: bfloat16 [768], P(('dp', 'fsdp')), may hold values from 0.5 to 1.5
- ln1_bias: bfloat16 [768], P(('dp', 'fsdp')), may hold values from -3 to 3
- w_qkv: bfloat16 [768, 2304], P(('dp', 'fsdp')), may hold values from -0.3125 to 0.3125
- w_out: bfloat16 [768, 768], P(('dp', 'fsdp')), may hold values from -2.5 to 2.5
- ln2_gain: bfloat16 [768], P(('dp', 'fsdp')), may hold values from 0.5 to 1.5
- ln2_bias: bfloat16 [768], P(('dp', 'fsdp')), may hold values from -3 to 3
- w_up: bfloat16 [768, 3072], P(('dp', 'fsdp')), may hold values from -0.21875 to 0.21875
- w_down: bfloat16 [3072, 768], P(('dp', 'fsdp')), may hold values from -0.75 to 0.75
Outputs:
- block_out: bfloat16 [64, 1024, 768], P('dp', 'fsdp')
- d_tokens: bfloat16 [64, 1024, 768], P('dp', 'fsdp')
- grad_ln1_gain: float32 [768], P(('dp', 'fsdp'))
- grad_ln1_bias: float32 [768], P(('dp', 'fsdp'))
- grad_w_qkv: float32 [768, 2304], P(('dp', 'fsdp'))
- grad_w_out: float32 [768, 768], P(('dp', 'fsdp'))
- grad_ln2_gain: float32 [768], P(('dp', 'fsdp'))
- grad_ln2_bias: float32 [768], P(('dp', 'fsdp'))
- grad_w_up: float32 [768, 3072], P(('dp', 'fsdp'))
- grad_w_down: float32 [3072, 768], P(('dp', 'fsdp'))
Inputs may be any that keep to these rules, and one draw needn't show every extreme that they name: lengths[g, p] is the live length of sequence perm[g, p] of dp group g, dealt to fsdp index p // 2 as its micro-batch p % 2; each row holds 1024 and 256 at least once. `perm`: each row is a permutation of the group's 8 sequences.
All inputs are finite; a program needn't handle non-finite values.
Results may differ from a plain program's by a relative error of at most 0.014.
The roundings to bfloat16 on the way count: a program that leaves them out, or rounds other values in their place, can miss the bound.
Values may be sent and summed in bfloat16 or wider, within the bound.
No kernel may reach another device: no remote copies, remote signals or barrier semaphores. Data moves between devices by JAX's collectives and lax.ppermute only.
A program may use at most 384 MiB of HBM per device.

v0:
```python
import math
import jax
import jax.numpy as jnp
from jax import lax
from jax.sharding import PartitionSpec as P

HEADS = 12
DEPTH = 48
epsilon = 1e-05


def gelu_tanh(value):
    inner = 0.7978845608028654 * (value + 0.044715 * value * value * value)
    return 0.5 * value * (1.0 + jnp.tanh(inner))


def norm_parts(seq_rows):
    center = seq_rows - jnp.mean(seq_rows, axis=-1, keepdims=True)
    factor = lax.rsqrt(jnp.mean(center * center, axis=-1, keepdims=True) + epsilon)
    return (center * factor, factor)


def norm_back(grad_normed, normed, factor, gain):
    grad_gain = jnp.sum(grad_normed * normed, axis=0)
    grad_bias = jnp.sum(grad_normed, axis=0)
    scaled = grad_normed * gain
    grad_rows = factor * (
        scaled
        - jnp.mean(scaled, axis=-1, keepdims=True)
        - normed * jnp.mean(scaled * normed, axis=-1, keepdims=True)
    )
    return (grad_rows, grad_gain, grad_bias)


def outer_sum(left, right):
    return lax.dot_general(
        left, right, (((0,), (0,)), ((), ())), preferred_element_type=jnp.float32
    )


def by_transpose(left, right):
    return lax.dot_general(
        left, right, (((1,), (1,)), ((), ())), preferred_element_type=jnp.float32
    )


def split_heads(qkv_low):
    row_count = qkv_low.shape[0]
    model_width = qkv_low.shape[1] // 3
    stacked = qkv_low.reshape(row_count, 3, HEADS, model_width // HEADS)
    return (stacked[:, 0], stacked[:, 1], stacked[:, 2])


def block_mask(first_row, block_rows, key_stop, seq_length):
    query_pos = first_row + lax.iota(jnp.int32, block_rows)
    key_pos = lax.iota(jnp.int32, key_stop)
    return (key_pos[None, :] <= query_pos[:, None]) & (key_pos[None, :] < seq_length)


def attend(qkv_low, seq_length):
    queries, key_rows, values = split_heads(qkv_low)
    row_count, head_count, head_size = queries.shape
    model_width = head_count * head_size
    block_rows = min(512, row_count)
    half_heads = head_count // 2
    factor = 1.0 / math.sqrt(head_size)
    mixed_parts = []
    total_parts = []
    for block_index in range(row_count // block_rows):
        first_row = block_index * block_rows
        key_stop = first_row + block_rows

        def compute(unused, first_row=first_row, key_stop=key_stop):
            allowed = block_mask(first_row, block_rows, key_stop, seq_length)
            query_block = queries[first_row:key_stop]
            outputs = []
            totals = []
            for half_index in range(2):
                low_head = half_index * half_heads
                high_head = low_head + half_heads
                scores = (
                    jnp.einsum(
                        "qhd,khd->hqk",
                        query_block[:, low_head:high_head],
                        key_rows[:key_stop, low_head:high_head],
                        preferred_element_type=jnp.float32,
                    )
                    * factor
                )
                scores = jnp.where(allowed[None], scores, -1e30)
                row_peak = jnp.max(scores, axis=-1, keepdims=True)
                exponent = jnp.exp(scores - row_peak)
                row_total = jnp.sum(exponent, axis=-1, keepdims=True)
                probs_low = (exponent / row_total).astype(jnp.bfloat16)
                outputs.append(
                    jnp.einsum(
                        "hqk,khd->qhd",
                        probs_low,
                        values[:key_stop, low_head:high_head],
                        preferred_element_type=jnp.float32,
                    )
                )
                totals.append((row_peak + jnp.log(row_total))[..., 0])
            return (
                jnp.concatenate(outputs, axis=1).reshape(block_rows, model_width),
                jnp.concatenate(totals, axis=0),
            )

        block_out, block_totals = compute(0)
        mixed_parts.append(block_out)
        total_parts.append(block_totals)
    return (jnp.concatenate(mixed_parts, axis=0), jnp.concatenate(total_parts, axis=1))


def attend_back(qkv_low, log_totals, grad_mixed, seq_length):
    queries, key_rows, values = split_heads(qkv_low)
    row_count, head_count, head_size = queries.shape
    grad_heads = grad_mixed.reshape(row_count, head_count, head_size)
    block_rows = min(512, row_count)
    half_heads = head_count // 2
    factor = 1.0 / math.sqrt(head_size)
    grad_keys = jnp.zeros((row_count, head_count, head_size), jnp.float32)
    grad_values = jnp.zeros((row_count, head_count, head_size), jnp.float32)
    query_parts = []
    for block_index in range(row_count // block_rows):
        first_row = block_index * block_rows
        key_stop = first_row + block_rows

        def compute(unused, first_row=first_row, key_stop=key_stop):
            allowed = block_mask(first_row, block_rows, key_stop, seq_length)
            query_block = queries[first_row:key_stop]
            grad_block = grad_heads[first_row:key_stop]
            query_list = []
            key_list = []
            value_list = []
            for half_index in range(2):
                low_head = half_index * half_heads
                high_head = low_head + half_heads
                scores = (
                    jnp.einsum(
                        "qhd,khd->hqk",
                        query_block[:, low_head:high_head],
                        key_rows[:key_stop, low_head:high_head],
                        preferred_element_type=jnp.float32,
                    )
                    * factor
                )
                scores = jnp.where(allowed[None], scores, -1e30)
                attn_probs = jnp.exp(
                    scores - log_totals[low_head:high_head, first_row:key_stop][..., None]
                )
                grad_probs = jnp.einsum(
                    "qhd,khd->hqk",
                    grad_block[:, low_head:high_head],
                    values[:key_stop, low_head:high_head],
                    preferred_element_type=jnp.float32,
                )
                inner = jnp.sum(attn_probs * grad_probs, axis=-1, keepdims=True)
                grad_scores = (attn_probs * (grad_probs - inner)).astype(jnp.bfloat16)
                query_list.append(
                    jnp.einsum(
                        "hqk,khd->qhd",
                        grad_scores,
                        key_rows[:key_stop, low_head:high_head],
                        preferred_element_type=jnp.float32,
                    )
                    * factor
                )
                key_list.append(
                    jnp.einsum(
                        "hqk,qhd->khd",
                        grad_scores,
                        query_block[:, low_head:high_head],
                        preferred_element_type=jnp.float32,
                    )
                    * factor
                )
                value_list.append(
                    jnp.einsum(
                        "hqk,qhd->khd",
                        attn_probs.astype(jnp.bfloat16),
                        grad_block[:, low_head:high_head],
                        preferred_element_type=jnp.float32,
                    )
                )
            return (
                jnp.concatenate(query_list, axis=1),
                jnp.concatenate(key_list, axis=1),
                jnp.concatenate(value_list, axis=1),
            )

        query_grad, key_grad, value_grad = compute(0)
        query_parts.append(query_grad)
        padding = ((0, row_count - key_stop), (0, 0), (0, 0))
        grad_keys = grad_keys + jnp.pad(key_grad, padding)
        grad_values = grad_values + jnp.pad(value_grad, padding)
    grad_queries = jnp.concatenate(query_parts, axis=0)
    return jnp.concatenate(
        [
            grad_queries.reshape(row_count, -1),
            grad_keys.reshape(row_count, -1),
            grad_values.reshape(row_count, -1),
        ],
        axis=1,
    )


def forward_one(weights, seq_rows, seq_length):
    gain_one, bias_one, qkv_weight, out_weight, gain_two, bias_two, up_weight, down_weight = weights
    branch = 1.0 / math.sqrt(DEPTH)
    live_rows = (lax.iota(jnp.int32, seq_rows.shape[0]) < seq_length)[:, None]
    resid = seq_rows.astype(jnp.float32)
    normed_one, factor_one = norm_parts(resid)
    first_low = (normed_one * gain_one.astype(jnp.float32) + bias_one.astype(jnp.float32)).astype(
        jnp.bfloat16
    )
    qkv_low = jnp.dot(first_low, qkv_weight, preferred_element_type=jnp.float32).astype(
        jnp.bfloat16
    )
    mixed_rows, log_totals = attend(qkv_low, seq_length)
    attn_low = mixed_rows.astype(jnp.bfloat16)
    middle = resid + branch * jnp.dot(attn_low, out_weight, preferred_element_type=jnp.float32)
    normed_two, factor_two = norm_parts(middle)
    second_low = (normed_two * gain_two.astype(jnp.float32) + bias_two.astype(jnp.float32)).astype(
        jnp.bfloat16
    )
    up_proj = jnp.dot(second_low, up_weight, preferred_element_type=jnp.float32)
    gelu_low = gelu_tanh(up_proj).astype(jnp.bfloat16)
    final_rows = middle + branch * jnp.dot(
        gelu_low, down_weight, preferred_element_type=jnp.float32
    )
    block_out = jnp.where(live_rows, final_rows, 0.0).astype(jnp.bfloat16)
    return (block_out, (first_low, qkv_low, log_totals, attn_low, middle, second_low, up_proj))


def backward_one(weights, seq_rows, seq_cotan, seq_length, kept):
    gain_one, bias_one, qkv_weight, out_weight, gain_two, bias_two, up_weight, down_weight = weights
    first_low, qkv_low, log_totals, attn_low, middle, second_low, up_proj = kept
    branch = 1.0 / math.sqrt(DEPTH)
    live_rows = (lax.iota(jnp.int32, seq_rows.shape[0]) < seq_length)[:, None]
    grad_out = jnp.where(live_rows, seq_cotan.astype(jnp.float32), 0.0)
    grad_mlp = (branch * grad_out).astype(jnp.bfloat16)
    gelu_low = gelu_tanh(up_proj).astype(jnp.bfloat16)
    grad_down = outer_sum(gelu_low, grad_mlp)
    grad_gelu = by_transpose(grad_mlp, down_weight)
    unused_value, gelu_pull = jax.vjp(gelu_tanh, up_proj)
    grad_up = gelu_pull(grad_gelu)[0].astype(jnp.bfloat16)
    grad_up_weight = outer_sum(second_low, grad_up)
    grad_second = by_transpose(grad_up, up_weight)
    normed_two, factor_two = norm_parts(middle)
    grad_middle_norm, grad_gain_two, grad_bias_two = norm_back(
        grad_second, normed_two, factor_two, gain_two.astype(jnp.float32)
    )
    grad_middle = grad_out + grad_middle_norm
    grad_attn_out = (branch * grad_middle).astype(jnp.bfloat16)
    grad_out_weight = outer_sum(attn_low, grad_attn_out)
    grad_mixed = by_transpose(grad_attn_out, out_weight).astype(jnp.bfloat16)
    grad_qkv = attend_back(qkv_low, log_totals, grad_mixed, seq_length).astype(jnp.bfloat16)
    grad_qkv_weight = outer_sum(first_low, grad_qkv)
    grad_first = by_transpose(grad_qkv, qkv_weight)
    normed_one, factor_one = norm_parts(seq_rows.astype(jnp.float32))
    grad_input_norm, grad_gain_one, grad_bias_one = norm_back(
        grad_first, normed_one, factor_one, gain_one.astype(jnp.float32)
    )
    grad_rows = (grad_middle + grad_input_norm).astype(jnp.bfloat16)
    return (
        grad_rows,
        (
            grad_gain_one,
            grad_bias_one,
            grad_qkv_weight,
            grad_out_weight,
            grad_gain_two,
            grad_bias_two,
            grad_up_weight,
            grad_down,
        ),
    )


def per_device(
    tokens,
    cotangent,
    lengths,
    perm,
    ln1_gain,
    ln1_bias,
    w_qkv,
    w_out,
    ln2_gain,
    ln2_bias,
    w_up,
    w_down,
):
    group_size = lax.axis_size("fsdp")
    slot_count = tokens.shape[0]
    micro_count = slot_count // group_size
    dealing = perm[0]
    own_lengths = lax.dynamic_slice_in_dim(
        lengths[0], lax.axis_index("fsdp") * micro_count, micro_count
    )
    dealt_rows = jnp.take(tokens, dealing, axis=0)
    dealt_grads = jnp.take(cotangent, dealing, axis=0)
    seq_tokens, seq_cotan = (
        lax.all_to_all(dealt_rows, "fsdp", split_axis=0, concat_axis=1, tiled=True),
        lax.all_to_all(dealt_grads, "fsdp", split_axis=0, concat_axis=1, tiled=True),
    )
    shards = (ln1_gain, ln1_bias, w_qkv, w_out, ln2_gain, ln2_bias, w_up, w_down)
    gathered = (
        lax.all_gather(shards[0], ("dp", "fsdp"), axis=0, tiled=True),
        lax.all_gather(shards[1], ("dp", "fsdp"), axis=0, tiled=True),
        lax.all_gather(shards[2], ("dp", "fsdp"), axis=0, tiled=True),
        lax.all_gather(shards[3], ("dp", "fsdp"), axis=0, tiled=True),
        lax.all_gather(shards[4], ("dp", "fsdp"), axis=0, tiled=True),
        lax.all_gather(shards[5], ("dp", "fsdp"), axis=0, tiled=True),
        lax.all_gather(shards[6], ("dp", "fsdp"), axis=0, tiled=True),
        lax.all_gather(shards[7], ("dp", "fsdp"), axis=0, tiled=True),
    )

    def forward_step(scan_carry, scan_item):
        block_out, kept = forward_one(gathered, scan_item[0], scan_item[1])
        return (scan_carry, (block_out, kept))

    unused_carry, (block_outs, kept_all) = lax.scan(
        forward_step, jnp.int32(0), (seq_tokens, own_lengths)
    )
    back_weights = (
        lax.all_gather(shards[0], ("dp", "fsdp"), axis=0, tiled=True),
        lax.all_gather(shards[1], ("dp", "fsdp"), axis=0, tiled=True),
        lax.all_gather(shards[2], ("dp", "fsdp"), axis=0, tiled=True),
        lax.all_gather(shards[3], ("dp", "fsdp"), axis=0, tiled=True),
        lax.all_gather(shards[4], ("dp", "fsdp"), axis=0, tiled=True),
        lax.all_gather(shards[5], ("dp", "fsdp"), axis=0, tiled=True),
        lax.all_gather(shards[6], ("dp", "fsdp"), axis=0, tiled=True),
        lax.all_gather(shards[7], ("dp", "fsdp"), axis=0, tiled=True),
    )

    def backward_step(totals, scan_item):
        grad_rows, additions = backward_one(
            back_weights, scan_item[0], scan_item[1], scan_item[2], scan_item[3]
        )
        return (tuple((left + right for left, right in zip(totals, additions))), grad_rows)

    zero_grads = tuple((jnp.zeros(piece.shape, jnp.float32) for piece in back_weights))
    totals, grad_tokens = lax.scan(
        backward_step, zero_grads, (seq_tokens, seq_cotan, own_lengths, kept_all), reverse=True
    )
    summed = lax.psum_scatter(totals, ("dp", "fsdp"), scatter_dimension=0, tiled=True)
    returned_out, returned_grad = (
        lax.all_to_all(block_outs, "fsdp", split_axis=1, concat_axis=0, tiled=True),
        lax.all_to_all(grad_tokens, "fsdp", split_axis=1, concat_axis=0, tiled=True),
    )
    inverse = jnp.zeros((slot_count,), jnp.int32).at[dealing].set(lax.iota(jnp.int32, slot_count))
    return (
        jnp.take(returned_out, inverse, axis=0),
        jnp.take(returned_grad, inverse, axis=0),
    ) + tuple(summed)


def solution(mesh):
    placed = (
        P("dp", "fsdp", None),
        P("dp", "fsdp", None),
        P("dp", None),
        P("dp", None),
        P(("dp", "fsdp")),
        P(("dp", "fsdp")),
        P(("dp", "fsdp"), None),
        P(("dp", "fsdp"), None),
        P(("dp", "fsdp")),
        P(("dp", "fsdp")),
        P(("dp", "fsdp"), None),
        P(("dp", "fsdp"), None),
    )
    return jax.shard_map(
        per_device,
        mesh=mesh,
        in_specs=placed,
        out_specs=(
            P("dp", "fsdp", None),
            P("dp", "fsdp", None),
            P(("dp", "fsdp")),
            P(("dp", "fsdp")),
            P(("dp", "fsdp"), None),
            P(("dp", "fsdp"), None),
            P(("dp", "fsdp")),
            P(("dp", "fsdp")),
            P(("dp", "fsdp"), None),
            P(("dp", "fsdp"), None),
        ),
        check_vma=False,
    )
```

profile of v0, /device:TPU:0, one launch (start us, length us, event | category | flops | bytes accessed | tf_op | source)
XLA Modules:
  0.0 1582.8 jit_solution(484979325144604657)
XLA Ops:
  17.0 5.2 broadcast_select_fusion.2
  22.2 6.3 all-to-all-start.2
  29.1 74.7 %all-to-all-done.2 = bf16[8,256,768]{2,1,0:T(8,128)(2,1)S(1)} async-done(((bf16[8,256,768]{2,1,0:T(8,128)(2,1)}), bf16[8,256,768]{2,1,0:T(8,128)(2,1)S(1)}, u32[]{:S(2)}, u32[]{:S(2)}) %all-to-all-start.2) | async-done | bytes 3145760 | tf_op jit(solution)/shard_map/all_to_all | solution.py:306
  103.9 4.8 all-to-all-start
  109.9 96.4 %all-reduce.11 = (bf16[768]{0:T(1024)(128)(2,1)S(1)}, bf16[768]{0:T(1024)(128)(2,1)S(1)}, bf16[768]{0:T(1024)(128)(2,1)S(1)}, bf16[768]{0:T(1024)(128)(2,1)S(1)}) all-reduce(bf16[768]{0:T(1024)(128)(2,1)S(1)} %dynamic-update-slice, bf16[768]{0:T(1024)(128)(2,1)S(1)} %dynamic-update-slice.1, ...), channel_id=1, replica_groups=mesh['dp'=8,'fsdp'=4] {'dp','fsdp'}, use_global_device_ids=true, to_apply=%add.2 | all-reduce | flops 3072 | bytes 12288
  210.9 62.9 %all-gather.9.cloned.1.call-done = bf16[768,3072]{1,0:T(8,128)(2,1)} async-done(((bf16[24,3072]{1,0:T(8,128)(2,1)}), bf16[768,3072]{1,0:T(8,128)(2,1)}) %all-gather.9.cloned.1.call-update) | async-done | bytes 4718608 | tf_op jit(solution)/shard_map/all_gather | solution.py:316
  273.7 64.6 %all-gather.11.cloned.1.call-done = bf16[3072,768]{1,0:T(8,128)(2,1)} async-done(((bf16[96,768]{1,0:T(8,128)(2,1)}), bf16[3072,768]{1,0:T(8,128)(2,1)}) %all-gather.11.cloned.1.call-update) | async-done | bytes 4718608 | tf_op jit(solution)/shard_map/all_gather | solution.py:317
  338.3 221.6 %while.55 = (s32[]{:T(128)}, bf16[2,1024,768]{1,2,0:T(8,128)(2,1)}, bf16[2,1024,768]{1,2,0:T(8,128)(2,1)}, bf16[2,1024,2304]{2,1,0:T(8,128)(2,1)}, f32[2,12,1024...) while((s32[]{:T(128)}, bf16[2,1024,768]{1,2,0:T(8,128)(2,1)}, ...), condition=%wide.region_13.15_spmd, body=%wide.region_0.14_spmd.sunk | while | flops 17094704128 | bytes 421247968 | solution.py:324
  368.3 8.6 bitcast_dynamic-update-slice_fusion.10
  376.9 6.7 copy.143
  396.0 6.2 fusion.362
  402.2 8.7 fusion.363
  411.0 6.5 fusion.366
  436.3 11.4 bitcast_dynamic-update-slice_fusion.11
  447.7 10.3 bitcast_dynamic-update-slice_fusion.12
  468.2 8.7 bitcast_dynamic-update-slice_fusion.10
  476.9 6.7 copy.143
  496.0 6.2 fusion.362
  502.2 8.7 fusion.363
  510.9 6.5 fusion.366
  536.2 11.6 bitcast_dynamic-update-slice_fusion.11
  547.9 10.3 bitcast_dynamic-update-slice_fusion.12
  561.8 450.0 %while.56 = (s32[]{:T(128)}, f32[768]{0:T(1024)}, f32[768]{0:T(1024)}, f32[768,2304]{1,0:T(8,128)}, f32[768,768]{1,0:T(8,128)}, /*index=5*/f32[768]{0:T(1024)}, ...) while((s32[]{:T(128)}, f32[768]{0:T(1024)}, ...), condition=%wide.region_32.34_spmd.clone, body=%wide.region_15.33_spmd.clone.sunk | while | flops 35389038592 | bytes 976789248 | solution.py:345
  584.3 5.5 constant_dynamic-slice_fusion.7
  589.7 6.7 copy.145
  602.1 19.4 %fusion.418 = bf16[1024,3072]{1,0:T(8,128)(2,1)} fusion(f32[2,1024,3072]{2,1,0:T(8,128)} %get-tuple-element.1590, s32[]{:T(128)S(6)} %sub.736, bf16[3072,768]{1,0:T(8,128)(2,1)} %get-tuple-element.1589, pred[1024]{0:T(1024)(128)(4,1)S(1)} %copy-done.73, bf16[2,1024,768]{2,1,0:T(8,128)(2,1)} %get-tuple-element.1587), kind=kOutput, calls=%fused_computation.129.clone.1 | convolution fusion | flops 4910481408 | bytes 25167872 | tf_op jit(solution)/shard_map/while/body/eval_jaxpr/dot_general | solution.py:42
  621.6 10.1 multiply_reduce_fusion.17
  643.6 7.5 select_add_fusion.18
  652.2 5.9 multiply_reduce_fusion.18
  658.1 7.3 multiply_convert_fusion.13
  675.5 13.4 select_add_fusion.19
  696.8 6.4 fusion.427
  703.2 6.4 fusion.429
  711.2 6.4 fusion.436
  717.6 18.3 %multiply_reduce_fusion.19 = (f32[6,512]{1,0:T(8,128)S(1)}, f32[6,512]{1,0:T(8,128)S(1)}, f32[6,512,1024]{2,1,0:T(8,128)}) fusion(f32[6,512,1024]{2,1,0:T(8,128)} %copy-done.12, f32[6,512]{1,0:T(8,128)S(1)} %copy-done.43, pred[512,1024]{1,0:T(8,128)(4,1)S(1)} %copy-done.19, f32[6,512,1024]{2,1,0:T(8,128)} %fusion.436, f32[6,512]{1,0:T(8,128)S(1)} %copy-done.45, ...), kind=kOutput, calls=%fused_computation.148.clone.1 | convolution fusion | flops 434104320 | bytes 52486144 | tf_op jit(solution)/shard_map/while/body/eval_jaxpr/qhd,khd->hqk/dot_general | solution.py:152
  735.8 17.5 %multiply_convert_fusion.14 = (bf16[6,512,1024]{2,1,0:T(8,128)(2,1)S(1)}, bf16[6,512,1024]{2,1,0:T(8,128)(2,1)S(1)}) fusion(f32[6,512,1024]{2,1,0:T(8,128)} %get-tuple-element.1440, f32[6,512,1024]{2,1,0:T(8,128)} %copy-done.12, f32[6,512]{1,0:T(8,128)S(1)} %get-tuple-element.1441, f32[6,512]{1,0:T(8,128)S(1)} %copy-done.43, ...), kind=kLoop, calls=%fused_computation.147.clone.1 | loop fusion | flops 37748736 | bytes 63488000 | tf_op jit(solution)/shard_map/while/body/eval_jaxpr/convert_element_type | solution.py:159
  765.5 7.0 fusion.442
  774.4 7.8 select_add_fusion.15
  799.4 5.5 constant_dynamic-slice_fusion.7
  804.9 6.7 copy.145
  817.3 19.5 %fusion.418 = bf16[1024,3072]{1,0:T(8,128)(2,1)} fusion(f32[2,1024,3072]{2,1,0:T(8,128)} %get-tuple-element.1590, s32[]{:T(128)S(6)} %sub.736, bf16[3072,768]{1,0:T(8,128)(2,1)} %get-tuple-element.1589, pred[1024]{0:T(1024)(128)(4,1)S(1)} %copy-done.73, bf16[2,1024,768]{2,1,0:T(8,128)(2,1)} %get-tuple-element.1587), kind=kOutput, calls=%fused_computation.129.clone.1 | convolution fusion | flops 4910481408 | bytes 25167872 | tf_op jit(solution)/shard_map/while/body/eval_jaxpr/dot_general | solution.py:42
  836.8 10.1 multiply_reduce_fusion.17
  856.0 4.6 select_add_fusion.16
  860.7 9.9 select_add_fusion.18
  871.6 5.9 multiply_reduce_fusion.18
  877.6 7.3 multiply_convert_fusion.13
  894.9 14.8 select_add_fusion.19
  917.6 6.4 fusion.427
  924.0 6.4 fusion.429
  932.0 6.4 fusion.436
  938.4 18.3 %multiply_reduce_fusion.19 = (f32[6,512]{1,0:T(8,128)S(1)}, f32[6,512]{1,0:T(8,128)S(1)}, f32[6,512,1024]{2,1,0:T(8,128)}) fusion(f32[6,512,1024]{2,1,0:T(8,128)} %copy-done.12, f32[6,512]{1,0:T(8,128)S(1)} %copy-done.43, pred[512,1024]{1,0:T(8,128)(4,1)S(1)} %copy-done.19, f32[6,512,1024]{2,1,0:T(8,128)} %fusion.436, f32[6,512]{1,0:T(8,128)S(1)} %copy-done.45, ...), kind=kOutput, calls=%fused_computation.148.clone.1 | convolution fusion | flops 434104320 | bytes 52486144 | tf_op jit(solution)/shard_map/while/body/eval_jaxpr/qhd,khd->hqk/dot_general | solution.py:152
  956.7 17.5 %multiply_convert_fusion.14 = (bf16[6,512,1024]{2,1,0:T(8,128)(2,1)S(1)}, bf16[6,512,1024]{2,1,0:T(8,128)(2,1)S(1)}) fusion(f32[6,512,1024]{2,1,0:T(8,128)} %get-tuple-element.1440, f32[6,512,1024]{2,1,0:T(8,128)} %copy-done.12, f32[6,512]{1,0:T(8,128)S(1)} %get-tuple-element.1441, f32[6,512]{1,0:T(8,128)S(1)} %copy-done.43, ...), kind=kLoop, calls=%fused_computation.147.clone.1 | loop fusion | flops 37748736 | bytes 63488000 | tf_op jit(solution)/shard_map/while/body/eval_jaxpr/convert_element_type | solution.py:159
  986.3 7.0 fusion.442
  995.2 7.8 select_add_fusion.15
  1015.1 4.9 copy.119
  1023.7 8.8 copy.110
  1032.5 68.9 %all-to-all-done.3 = bf16[2,1024,768]{2,0,1:T(2,128)(2,1)S(1)} async-done(((bf16[2,1024,768]{2,0,1:T(2,128)(2,1)}), bf16[2,1024,768]{2,0,1:T(2,128)(2,1)S(1)}, u32[]{:S(2)}, u32[]{:S(2)}) %all-to-all-start.3) | async-done | bytes 3145760 | tf_op jit(solution)/shard_map/all_to_all | solution.py:351
  1101.4 4.7 all-to-all-start.1
  1106.8 93.8 %all-reduce.10 = (f32[768]{0:T(1024)S(1)}, f32[768]{0:T(1024)S(1)}, f32[768]{0:T(1024)S(1)}, f32[768]{0:T(1024)S(1)}) all-reduce(f32[768]{0:T(1024)S(1)} %copy-done.71, f32[768]{0:T(1024)S(1)} %copy-done.68, f32[768]{0:T(1024)S(1)} %copy-done.65, f32[768]{0:T(1024)S(1)} %get-tuple-element.640), channel_id=2, replica_groups=mesh['dp'=8,'fsdp'=4] {'dp','fsdp'}, use_global_device_ids=true, to_apply=%region_33.35.clone | all-reduce | flops 3072 | bytes 24576
  1210.3 4.5 gather_fusion.1
  1214.9 6.3 broadcast_select_fusion
  1221.2 71.3 %reduce-scatter.5.cloned.1.call-done = f32[24,2304]{1,0:T(8,128)} async-done(((f32[768,2304]{1,0:T(8,128)}), f32[24,2304]{1,0:T(8,128)}) %reduce-scatter.5.cloned.1.call-update) | async-done | bytes 221200 | tf_op jit(solution)/shard_map/reduce_scatter | solution.py:348
  1292.4 141.6 %reduce-scatter.9.cloned.1.call-done = f32[24,3072]{1,0:T(8,128)} async-done(((f32[768,3072]{1,0:T(8,128)}), f32[24,3072]{1,0:T(8,128)}) %reduce-scatter.9.cloned.1.call-update) | async-done | bytes 294928 | tf_op jit(solution)/shard_map/reduce_scatter | solution.py:348
  1434.1 141.6 %reduce-scatter.11.cloned.1.call-done = f32[96,768]{1,0:T(8,128)} async-done(((f32[3072,768]{1,0:T(8,128)}), f32[96,768]{1,0:T(8,128)}) %reduce-scatter.11.cloned.1.call-update) | async-done | bytes 294928 | tf_op jit(solution)/shard_map/reduce_scatter | solution.py:348
  (633 shorter events, 251.2 us)
Async XLA Ops:
  7.2 203.7 %all-gather.7.cloned.1.call-start = ((), (), s32[]{:S(2)}) async-start(), calls=%async_computation.9 | async-start | bytes 1216512 | tf_op jit(solution)/shard_map/all_gather | solution.py:313
  7.9 203.0 %all-gather.5.cloned.1.call-start = ((), (), s32[]{:S(2)}) async-start(), calls=%async_computation.8 | async-start | bytes 3649536 | tf_op jit(solution)/shard_map/all_gather | solution.py:312
  8.7 265.1 %all-gather.9.cloned.1.call-start = ((), (), s32[]{:S(2)}) async-start(), calls=%async_computation.10 | async-start | bytes 4866048 | tf_op jit(solution)/shard_map/all_gather | solution.py:316
  22.2 81.7 %all-to-all-start.2 = ((bf16[8,256,768]{2,1,0:T(8,128)(2,1)}), bf16[8,256,768]{2,1,0:T(8,128)(2,1)S(1)}, u32[]{:S(2)}, u32[]{:S(2)}) async-start(bf16[8,256,768]{2,1,0:T(8,128)(2,1)} %get-tuple-element.1064), calls=%async_computation.2 | async-start | bytes 6291456 | tf_op jit(solution)/shard_map/all_to_all | solution.py:306
  28.6 309.8 %all-gather.11.cloned.1.call-start = ((), (), s32[]{:S(2)}) async-start(), calls=%async_computation.11 | async-start | bytes 4866048 | tf_op jit(solution)/shard_map/all_gather | solution.py:317
  103.9 102.4 %copy-start.91 = (s32[1,8]{1,0:T(1,128)S(1)}, s32[1,8]{1,0:T(1,128)}, u32[]{:S(2)}) copy-start(s32[1,8]{1,0:T(1,128)} %param.20) | copy-start | bytes 100
  103.9 104.9 %all-to-all-start = ((bf16[8,256,768]{2,1,0:T(8,128)(2,1)}), bf16[8,256,768]{2,1,0:T(8,128)(2,1)}, u32[]{:S(2)}, u32[]{:S(2)}) async-start(bf16[8,256,768]{2,1,0:T(8,128)(2,1)} %get-tuple-element.1065), calls=%async_computation | async-start | bytes 6291456 | tf_op jit(solution)/shard_map/all_to_all | solution.py:305
  108.7 1112.5 %reduce-scatter.7.cloned.1.call-start = ((), (), s32[]{:S(2)}) async-start(), calls=%async_computation.13 | async-start | bytes 2433024 | tf_op jit(solution)/shard_map/reduce_scatter | solution.py:348
  428.6 7.7 slice-start.4
  436.3 11.4 copy-start.40
  436.3 11.4 copy-start.79
  447.7 12.0 copy-start.8
  447.7 12.0 copy-start.53
  447.7 12.0 copy-start.57
  447.7 12.0 copy-start.75
  447.7 12.0 copy-start.77
  528.5 7.7 slice-start.4
  536.2 11.6 copy-start.40
  536.2 11.6 copy-start.79
  547.8 12.0 copy-start.8
  547.8 12.0 copy-start.53
  547.9 12.0 copy-start.57
  547.9 12.0 copy-start.75
  547.9 12.0 copy-start.77
  570.2 11.1 copy-start.9
  583.8 12.7 copy-start.4
  600.1 72.0 %copy-start.15 = (bf16[1024,12,64]{0,2,1:T(8,128)(2,1)}, bf16[1024,12,64]{0,2,1:T(8,128)(2,1)S(1)}, u32[]{:S(2)}) copy-start(bf16[1024,12,64]{0,2,1:T(8,128)(2,1)S(1)} %get-tuple-element.1428) | copy-start | bytes 4718596 | tf_op jit(solution)/shard_map/while
  621.6 10.1 copy-start.5
  621.6 10.1 copy-start.24
  635.9 7.8 slice-start.8
  643.6 7.5 copy-start.17
  665.5 8.0 slice-start
  761.1 13.3 slice-start.6
  765.5 8.9 slice-start.7
  774.4 7.9 copy-start.36
  774.4 10.8 copy-start.49
  774.4 10.8 copy-start.55
  774.4 10.8 copy-start.59
  774.4 10.8 copy-start.62
  785.4 11.1 copy-start.9
  798.9 12.7 copy-start.4
  815.2 76.3 %copy-start.15 = (bf16[1024,12,64]{0,2,1:T(8,128)(2,1)}, bf16[1024,12,64]{0,2,1:T(8,128)(2,1)S(1)}, u32[]{:S(2)}) copy-start(bf16[1024,12,64]{0,2,1:T(8,128)(2,1)S(1)} %get-tuple-element.1428) | copy-start | bytes 4718596 | tf_op jit(solution)/shard_map/while
  836.8 10.1 copy-start.5
  836.8 10.1 copy-start.24
  851.1 9.6 slice-start.8
  860.7 9.9 copy-start.17
  884.9 8.0 slice-start
  981.9 13.3 slice-start.6
  986.3 8.9 slice-start.7
  995.2 7.9 copy-start.36
  995.2 10.8 copy-start.49
  995.2 10.8 copy-start.55
  995.2 10.8 copy-start.59
  995.2 10.8 copy-start.62
  1011.9 280.6 %reduce-scatter.5.cloned.1.call-start = ((), (), s32[]{:S(2)}) async-start(), calls=%async_computation.12 | async-start | bytes 7299072 | tf_op jit(solution)/shard_map/reduce_scatter | solution.py:348
  1012.4 421.6 %reduce-scatter.9.cloned.1.call-start = ((), (), s32[]{:S(2)}) async-start(), calls=%async_computation.14 | async-start | bytes 9732096 | tf_op jit(solution)/shard_map/reduce_scatter | solution.py:348
  1013.2 562.5 %reduce-scatter.11.cloned.1.call-start = ((), (), s32[]{:S(2)}) async-start(), calls=%async_computation.15 | async-start | bytes 9732096 | tf_op jit(solution)/shard_map/reduce_scatter | solution.py:348
  1020.0 81.4 %all-to-all-start.3 = ((bf16[2,1024,768]{2,0,1:T(2,128)(2,1)}), bf16[2,1024,768]{2,0,1:T(2,128)(2,1)S(1)}, u32[]{:S(2)}, u32[]{:S(2)}) async-start(bf16[2,1024,768]{2,0,1:T(2,128)(2,1)} %copy.119), calls=%async_computation.3 | async-start | bytes 6291456 | tf_op jit(solution)/shard_map/all_to_all | solution.py:351
  1032.5 73.6 %copy-start.93 = (s32[1,8]{1,0:T(1,128)S(1)}, s32[1,8]{1,0:T(1,128)}, u32[]{:S(2)}) copy-start(s32[1,8]{1,0:T(1,128)} %param.21) | copy-start | bytes 100
  1032.5 74.3 %copy-start.65 = (f32[768]{0:T(1024)S(1)}, f32[768]{0:T(1024)}, u32[]{:S(2)}) copy-start(f32[768]{0:T(1024)} %get-tuple-element.639) | copy-start | bytes 9220
  1032.5 74.3 %copy-start.68 = (f32[768]{0:T(1024)S(1)}, f32[768]{0:T(1024)}, u32[]{:S(2)}) copy-start(f32[768]{0:T(1024)} %get-tuple-element.636) | copy-start | bytes 9220
  1032.5 74.3 %copy-start.71 = (f32[768]{0:T(1024)S(1)}, f32[768]{0:T(1024)}, u32[]{:S(2)}) copy-start(f32[768]{0:T(1024)} %get-tuple-element.635) | copy-start | bytes 9220
  1101.4 102.2 %all-to-all-start.1 = ((bf16[2,1024,768]{2,0,1:T(2,128)(2,1)}), bf16[2,1024,768]{2,0,1:T(2,128)(2,1)}, u32[]{:S(2)}, u32[]{:S(2)}) async-start(bf16[2,1024,768]{2,0,1:T(2,128)(2,1)} %copy.110), calls=%async_computation.1 | async-start | bytes 6291456 | tf_op jit(solution)/shard_map/all_to_all | solution.py:350
  1214.9 360.9 %copy-start.1 = (bf16[8,256,768]{2,1,0:T(8,128)(2,1)S(1)}, bf16[8,256,768]{2,1,0:T(8,128)(2,1)}, u32[]{:S(2)}) copy-start(bf16[8,256,768]{2,1,0:T(8,128)(2,1)} %param.19) | copy-start | bytes 9437188
  (141 other events, 491.0 us)
Sparse Core Ops, SparseCore 0:
  10.8 97.0 all-gather.6
  110.7 97.8 all-gather.4
  211.3 62.3 all-gather.8
  276.4 61.8 all-gather.10
  1012.0 153.8 reduce-scatter.6
  1172.0 120.4 reduce-scatter.4
  1298.9 135.1 reduce-scatter.8
  1440.6 135.1 reduce-scatter.10
where the time goes:
time: 1590 us; the launch traced here: 1580 us
  waiting for transfers between devices  630 us (40%)
  matrix products  427 us (27%)
  blocking collectives  190 us (12%)
  local copies, waits for them, and re-layouts  150 us (9%)
  other arithmetic  112 us (7%)
  loops' own time  38.4 us (2%)
  starting transfers between devices  19.8 us (1%)
    reduce_scatter x4, waiting for transfers between devices, per_device(): lax.psum_scatter(totals, ('dp', 'fsdp'), scatter_dimension=0, tiled=True)  355 us
    unnamed x2, blocking collectives  190 us
    dot_general x8, matrix products, by_transpose(): lax.dot_general(left, right, (((1,), (1,)), ((), ())), preferred_element_...  76.1 us
    all_to_all x1, waiting for transfers between devices, per_device(): lax.all_to_all(dealt_grads, 'fsdp', split_axis=0, concat_axis=1, tiled=True)  74.7 us
    all_to_all x1, waiting for transfers between devices, per_device(): lax.all_to_all(grad_tokens, 'fsdp', split_axis=1, concat_axis=0, tiled=True)  68.9 us
    dot_general x8, matrix products, outer_sum(): lax.dot_general(left, right, (((0,), (0,)), ((), ())), preferred_element_...  68.7 us
    all_gather x1, waiting for transfers between devices, per_device(): lax.all_gather(shards[7], ('dp', 'fsdp'), axis=0, tiled=True)  64.6 us
    dot_general x8, matrix products, compute(): jnp.einsum('qhd,khd->hqk', grad_block[:, low_head:high_head], values[:key...  63.3 us
  transfers between devices with their start and end apart: 12, of which 7 were waited for; matrix products, arithmetic and copies ran while one was open for 3% of the time, Pallas kernels for 0%

commit v1 on v0

--- a/solution.py
+++ b/solution.py
@@ -303,7 +303,12 @@
     dealt_grads = jnp.take(cotangent, dealing, axis=0)
     seq_tokens, seq_cotan = (
         lax.all_to_all(dealt_rows, "fsdp", split_axis=0, concat_axis=1, tiled=True),
-        lax.all_to_all(dealt_grads, "fsdp", split_axis=0, concat_axis=1, tiled=True),
+        jnp.concatenate(
+            lax.all_to_all(
+                jnp.stack(jnp.split(dealt_grads, lax.axis_size("fsdp"), axis=0)), "fsdp", 0, 0
+            ),
+            axis=1,
+        ),
     )
     shards = (ln1_gain, ln1_bias, w_qkv, w_out, ln2_gain, ln2_bias, w_up, w_down)
     gathered = (

time: 1590 us -> 1580 us (level)
  waiting for transfers between devices: 630 us -> 611 us
    all_gather x1, waiting for transfers between devices: 62.9 us -> 42.7 us  [per_device(): lax.all_gather(shards[6], ('dp', 'fsdp'), axis=0, tiled=True)]
where the time goes in v1:
time: 1580 us; the launch traced here: 1570 us
  waiting for transfers between devices  611 us (39%)
  matrix products  428 us (27%)
  blocking collectives  200 us (13%)
  local copies, waits for them, and re-layouts  150 us (9%)
  other arithmetic  113 us (7%)
  loops' own time  38.4 us (2%)
  starting transfers between devices  19.8 us (1%)
    reduce_scatter x4, waiting for transfers between devices, per_device(): lax.psum_scatter(totals, ('dp', 'fsdp'), scatter_dimension=0, tiled=True)  355 us
    unnamed x2, blocking collectives  200 us
    dot_general x8, matrix products, by_transpose(): lax.dot_general(left, right, (((1,), (1,)), ((), ())), preferred_element_...  76.1 us
    all_to_all x1, waiting for transfers between devices, per_device(): lax.all_to_all(jnp.stack(jnp.split(dealt_grads, lax.axis_size('fsdp'), ax...  75 us
    all_to_all x1, waiting for transfers between devices, per_device(): lax.all_to_all(grad_tokens, 'fsdp', split_axis=1, concat_axis=0, tiled=True)  68.9 us
    dot_general x8, matrix products, outer_sum(): lax.dot_general(left, right, (((0,), (0,)), ((), ())), preferred_element_...  68.9 us
    all_gather x1, waiting for transfers between devices, per_device(): lax.all_gather(shards[7], ('dp', 'fsdp'), axis=0, tiled=True)  64.6 us
    dot_general x8, matrix products, compute(): jnp.einsum('qhd,khd->hqk', grad_block[:, low_head:high_head], values[:key...  63.3 us
  transfers between devices with their start and end apart: 12, of which 7 were waited for; matrix products, arithmetic and copies ran while one was open for 3% of the time, Pallas kernels for 0%

profile of v1, /device:TPU:0, one launch (start us, length us, event | category | flops | bytes accessed | tf_op | source)
XLA Modules:
  0.0 1574.1 jit_solution(1618832858144463599)
XLA Ops:
  12.5 4.4 gather_fusion
  23.3 6.3 all-to-all-start.2
  30.2 75.0 %all-to-all-done.2 = bf16[4,2,256,768]{3,2,1,0:T(8,128)(2,1)S(1)} async-done(((bf16[4,2,256,768]{3,2,1,0:T(8,128)(2,1)}), bf16[4,2,256,768]{3,2,1,0:T(8,128)(2,1)S(1)}, u32[]{:S(2)}, u32[]{:S(2)}) %all-to-all-start.2) | async-done | bytes 3145760 | tf_op jit(solution)/shard_map/all_to_all | solution.py:307
  105.2 4.8 all-to-all-start
  111.2 106.0 %all-reduce.11 = (bf16[768]{0:T(1024)(128)(2,1)S(1)}, bf16[768]{0:T(1024)(128)(2,1)S(1)}, bf16[768]{0:T(1024)(128)(2,1)S(1)}, bf16[768]{0:T(1024)(128)(2,1)S(1)}) all-reduce(bf16[768]{0:T(1024)(128)(2,1)S(1)} %dynamic-update-slice, bf16[768]{0:T(1024)(128)(2,1)S(1)} %dynamic-update-slice.1, ...), channel_id=1, replica_groups=mesh['dp'=8,'fsdp'=4] {'dp','fsdp'}, use_global_device_ids=true, to_apply=%add.2 | all-reduce | flops 3072 | bytes 12288
  221.8 42.7 %all-gather.9.cloned.1.call-done = bf16[768,3072]{1,0:T(8,128)(2,1)} async-done(((bf16[24,3072]{1,0:T(8,128)(2,1)}), bf16[768,3072]{1,0:T(8,128)(2,1)}) %all-gather.9.cloned.1.call-update) | async-done | bytes 4718608 | tf_op jit(solution)/shard_map/all_gather | solution.py:321
  264.5 64.6 %all-gather.11.cloned.1.call-done = bf16[3072,768]{1,0:T(8,128)(2,1)} async-done(((bf16[96,768]{1,0:T(8,128)(2,1)}), bf16[3072,768]{1,0:T(8,128)(2,1)}) %all-gather.11.cloned.1.call-update) | async-done | bytes 4718608 | tf_op jit(solution)/shard_map/all_gather | solution.py:322
  329.1 221.5 %while.55 = (s32[]{:T(128)}, bf16[2,1024,768]{1,2,0:T(8,128)(2,1)}, bf16[2,1024,768]{1,2,0:T(8,128)(2,1)}, bf16[2,1024,2304]{2,1,0:T(8,128)(2,1)}, f32[2,12,1024...) while((s32[]{:T(128)}, bf16[2,1024,768]{1,2,0:T(8,128)(2,1)}, ...), condition=%wide.region_13.15_spmd, body=%wide.region_0.14_spmd.sunk | while | flops 17094704128 | bytes 421247968 | solution.py:329
  359.1 8.6 bitcast_dynamic-update-slice_fusion.10
  367.7 6.7 copy.143
  386.8 6.2 fusion.362
  392.9 8.7 fusion.363
  401.7 6.5 fusion.366
  427.0 11.4 bitcast_dynamic-update-slice_fusion.11
  438.5 10.3 bitcast_dynamic-update-slice_fusion.12
  459.0 8.7 bitcast_dynamic-update-slice_fusion.10
  467.6 6.7 copy.143
  486.7 6.2 fusion.362
  492.9 8.7 fusion.363
  501.7 6.5 fusion.366
  526.9 11.6 bitcast_dynamic-update-slice_fusion.11
  538.6 10.3 bitcast_dynamic-update-slice_fusion.12
  552.5 450.2 %while.56 = (s32[]{:T(128)}, f32[768]{0:T(1024)}, f32[768]{0:T(1024)}, f32[768,2304]{1,0:T(8,128)}, f32[768,768]{1,0:T(8,128)}, /*index=5*/f32[768]{0:T(1024)}, ...) while((s32[]{:T(128)}, f32[768]{0:T(1024)}, ...), condition=%wide.region_32.34_spmd.clone, body=%wide.region_15.33_spmd.clone.sunk | while | flops 35389038592 | bytes 976789248 | solution.py:350
  575.0 5.5 constant_dynamic-slice_fusion.7
  580.5 6.7 copy.145
  592.9 19.4 %fusion.418 = bf16[1024,3072]{1,0:T(8,128)(2,1)} fusion(f32[2,1024,3072]{2,1,0:T(8,128)} %get-tuple-element.1594, s32[]{:T(128)S(6)} %sub.736, bf16[3072,768]{1,0:T(8,128)(2,1)} %get-tuple-element.1593, pred[1024]{0:T(1024)(128)(4,1)S(1)} %copy-done.73, bf16[2,1024,768]{2,1,0:T(8,128)(2,1)} %get-tuple-element.1591), kind=kOutput, calls=%fused_computation.129.clone.1 | convolution fusion | flops 4910481408 | bytes 25167872 | tf_op jit(solution)/shard_map/while/body/eval_jaxpr/dot_general | solution.py:42
  612.3 10.1 multiply_reduce_fusion.17
  634.3 7.6 select_add_fusion.18
  643.0 5.9 multiply_reduce_fusion.18
  648.9 7.3 multiply_convert_fusion.13
  666.3 13.4 select_add_fusion.19
  687.6 6.4 fusion.427
  694.0 6.4 fusion.429
  702.0 6.4 fusion.436
  708.4 18.3 %multiply_reduce_fusion.19 = (f32[6,512]{1,0:T(8,128)S(1)}, f32[6,512]{1,0:T(8,128)S(1)}, f32[6,512,1024]{2,1,0:T(8,128)}) fusion(f32[6,512,1024]{2,1,0:T(8,128)} %copy-done.12, f32[6,512]{1,0:T(8,128)S(1)} %copy-done.43, pred[512,1024]{1,0:T(8,128)(4,1)S(1)} %copy-done.19, f32[6,512,1024]{2,1,0:T(8,128)} %fusion.436, f32[6,512]{1,0:T(8,128)S(1)} %copy-done.45, ...), kind=kOutput, calls=%fused_computation.148.clone.1 | convolution fusion | flops 434104320 | bytes 52486144 | tf_op jit(solution)/shard_map/while/body/eval_jaxpr/qhd,khd->hqk/dot_general | solution.py:152
  726.7 17.5 %multiply_convert_fusion.14 = (bf16[6,512,1024]{2,1,0:T(8,128)(2,1)S(1)}, bf16[6,512,1024]{2,1,0:T(8,128)(2,1)S(1)}) fusion(f32[6,512,1024]{2,1,0:T(8,128)} %get-tuple-element.1444, f32[6,512,1024]{2,1,0:T(8,128)} %copy-done.12, f32[6,512]{1,0:T(8,128)S(1)} %get-tuple-element.1445, f32[6,512]{1,0:T(8,128)S(1)} %copy-done.43, ...), kind=kLoop, calls=%fused_computation.147.clone.1 | loop fusion | flops 37748736 | bytes 63488000 | tf_op jit(solution)/shard_map/while/body/eval_jaxpr/convert_element_type | solution.py:159
  756.3 7.0 fusion.442
  765.2 7.8 select_add_fusion.15
  790.2 5.5 constant_dynamic-slice_fusion.7
  795.7 6.7 copy.145
  808.1 19.5 %fusion.418 = bf16[1024,3072]{1,0:T(8,128)(2,1)} fusion(f32[2,1024,3072]{2,1,0:T(8,128)} %get-tuple-element.1594, s32[]{:T(128)S(6)} %sub.736, bf16[3072,768]{1,0:T(8,128)(2,1)} %get-tuple-element.1593, pred[1024]{0:T(1024)(128)(4,1)S(1)} %copy-done.73, bf16[2,1024,768]{2,1,0:T(8,128)(2,1)} %get-tuple-element.1591), kind=kOutput, calls=%fused_computation.129.clone.1 | convolution fusion | flops 4910481408 | bytes 25167872 | tf_op jit(solution)/shard_map/while/body/eval_jaxpr/dot_general | solution.py:42
  827.6 10.1 multiply_reduce_fusion.17
  846.8 4.6 select_add_fusion.16
  851.4 10.0 select_add_fusion.18
  862.5 5.9 multiply_reduce_fusion.18
  868.4 7.3 multiply_convert_fusion.13
  885.8 14.8 select_add_fusion.19
  908.4 6.4 fusion.427
  914.9 6.4 fusion.429
  922.8 6.4 fusion.436
  929.2 18.3 %multiply_reduce_fusion.19 = (f32[6,512]{1,0:T(8,128)S(1)}, f32[6,512]{1,0:T(8,128)S(1)}, f32[6,512,1024]{2,1,0:T(8,128)}) fusion(f32[6,512,1024]{2,1,0:T(8,128)} %copy-done.12, f32[6,512]{1,0:T(8,128)S(1)} %copy-done.43, pred[512,1024]{1,0:T(8,128)(4,1)S(1)} %copy-done.19, f32[6,512,1024]{2,1,0:T(8,128)} %fusion.436, f32[6,512]{1,0:T(8,128)S(1)} %copy-done.45, ...), kind=kOutput, calls=%fused_computation.148.clone.1 | convolution fusion | flops 434104320 | bytes 52486144 | tf_op jit(solution)/shard_map/while/body/eval_jaxpr/qhd,khd->hqk/dot_general | solution.py:152
  947.5 17.5 %multiply_convert_fusion.14 = (bf16[6,512,1024]{2,1,0:T(8,128)(2,1)S(1)}, bf16[6,512,1024]{2,1,0:T(8,128)(2,1)S(1)}) fusion(f32[6,512,1024]{2,1,0:T(8,128)} %get-tuple-element.1444, f32[6,512,1024]{2,1,0:T(8,128)} %copy-done.12, f32[6,512]{1,0:T(8,128)S(1)} %get-tuple-element.1445, f32[6,512]{1,0:T(8,128)S(1)} %copy-done.43, ...), kind=kLoop, calls=%fused_computation.147.clone.1 | loop fusion | flops 37748736 | bytes 63488000 | tf_op jit(solution)/shard_map/while/body/eval_jaxpr/convert_element_type | solution.py:159
  977.2 7.0 fusion.442
  986.1 7.8 select_add_fusion.15
  1006.0 4.9 copy.119
  1014.6 8.8 copy.110
  1023.4 68.9 %all-to-all-done.3 = bf16[2,1024,768]{2,0,1:T(2,128)(2,1)S(1)} async-done(((bf16[2,1024,768]{2,0,1:T(2,128)(2,1)}), bf16[2,1024,768]{2,0,1:T(2,128)(2,1)S(1)}, u32[]{:S(2)}, u32[]{:S(2)}) %all-to-all-start.3) | async-done | bytes 3145760 | tf_op jit(solution)/shard_map/all_to_all | solution.py:356
  1092.3 4.7 all-to-all-start.1
  1097.7 93.8 %all-reduce.10 = (f32[768]{0:T(1024)S(1)}, f32[768]{0:T(1024)S(1)}, f32[768]{0:T(1024)S(1)}, f32[768]{0:T(1024)S(1)}) all-reduce(f32[768]{0:T(1024)S(1)} %copy-done.71, f32[768]{0:T(1024)S(1)} %copy-done.68, f32[768]{0:T(1024)S(1)} %copy-done.65, f32[768]{0:T(1024)S(1)} %get-tuple-element.640), channel_id=2, replica_groups=mesh['dp'=8,'fsdp'=4] {'dp','fsdp'}, use_global_device_ids=true, to_apply=%region_33.35.clone | all-reduce | flops 3072 | bytes 24576
  1201.2 4.5 gather_fusion.1
  1205.7 6.3 broadcast_select_fusion
  1212.0 71.3 %reduce-scatter.5.cloned.1.call-done = f32[24,2304]{1,0:T(8,128)} async-done(((f32[768,2304]{1,0:T(8,128)}), f32[24,2304]{1,0:T(8,128)}) %reduce-scatter.5.cloned.1.call-update) | async-done | bytes 221200 | tf_op jit(solution)/shard_map/reduce_scatter | solution.py:353
  1283.3 141.8 %reduce-scatter.9.cloned.1.call-done = f32[24,3072]{1,0:T(8,128)} async-done(((f32[768,3072]{1,0:T(8,128)}), f32[24,3072]{1,0:T(8,128)}) %reduce-scatter.9.cloned.1.call-update) | async-done | bytes 294928 | tf_op jit(solution)/shard_map/reduce_scatter | solution.py:353
  1425.1 141.9 %reduce-scatter.11.cloned.1.call-done = f32[96,768]{1,0:T(8,128)} async-done(((f32[3072,768]{1,0:T(8,128)}), f32[96,768]{1,0:T(8,128)}) %reduce-scatter.11.cloned.1.call-update) | async-done | bytes 294928 | tf_op jit(solution)/shard_map/reduce_scatter | solution.py:353
  (635 shorter events, 252.9 us)
Async XLA Ops:
  7.2 214.6 %all-gather.7.cloned.1.call-start = ((), (), s32[]{:S(2)}) async-start(), calls=%async_computation.9 | async-start | bytes 1216512 | tf_op jit(solution)/shard_map/all_gather | solution.py:318
  7.9 213.9 %all-gather.5.cloned.1.call-start = ((), (), s32[]{:S(2)}) async-start(), calls=%async_computation.8 | async-start | bytes 3649536 | tf_op jit(solution)/shard_map/all_gather | solution.py:317
  8.7 255.9 %all-gather.9.cloned.1.call-start = ((), (), s32[]{:S(2)}) async-start(), calls=%async_computation.10 | async-start | bytes 4866048 | tf_op jit(solution)/shard_map/all_gather | solution.py:321
  23.3 81.9 %all-to-all-start.2 = ((bf16[4,2,256,768]{3,2,1,0:T(8,128)(2,1)}), bf16[4,2,256,768]{3,2,1,0:T(8,128)(2,1)S(1)}, u32[]{:S(2)}, u32[]{:S(2)}) async-start(bf16[4,2,256,768]{3,2,1,0:T(8,128)(2,1)} %pad_maximum_fusion.3), calls=%async_computation.2 | async-start | bytes 6291456 | tf_op jit(solution)/shard_map/all_to_all | solution.py:307
  29.6 299.5 %all-gather.11.cloned.1.call-start = ((), (), s32[]{:S(2)}) async-start(), calls=%async_computation.11 | async-start | bytes 4866048 | tf_op jit(solution)/shard_map/all_gather | solution.py:322
  105.2 112.0 %copy-start.91 = (s32[1,8]{1,0:T(1,128)S(1)}, s32[1,8]{1,0:T(1,128)}, u32[]{:S(2)}) copy-start(s32[1,8]{1,0:T(1,128)} %param.20) | copy-start | bytes 100
  105.2 114.5 %all-to-all-start = ((bf16[8,256,768]{2,1,0:T(8,128)(2,1)}), bf16[8,256,768]{2,1,0:T(8,128)(2,1)}, u32[]{:S(2)}, u32[]{:S(2)}) async-start(bf16[8,256,768]{2,1,0:T(8,128)(2,1)} %get-tuple-element.1069), calls=%async_computation | async-start | bytes 6291456 | tf_op jit(solution)/shard_map/all_to_all | solution.py:305
  110.0 1102.0 %reduce-scatter.7.cloned.1.call-start = ((), (), s32[]{:S(2)}) async-start(), calls=%async_computation.13 | async-start | bytes 2433024 | tf_op jit(solution)/shard_map/reduce_scatter | solution.py:353
  419.3 7.7 slice-start.4
  427.0 11.4 copy-start.40
  427.0 11.4 copy-start.79
  438.5 12.0 copy-start.8
  438.5 12.0 copy-start.53
  438.5 12.0 copy-start.57
  438.5 12.0 copy-start.75
  438.5 12.0 copy-start.77
  519.3 7.6 slice-start.4
  526.9 11.6 copy-start.40
  526.9 11.6 copy-start.79
  538.6 12.0 copy-start.8
  538.6 12.0 copy-start.53
  538.6 12.0 copy-start.57
  538.6 12.0 copy-start.75
  538.6 12.0 copy-start.77
  561.0 11.1 copy-start.9
  574.5 12.6 copy-start.4
  590.8 72.1 %copy-start.15 = (bf16[1024,12,64]{0,2,1:T(8,128)(2,1)}, bf16[1024,12,64]{0,2,1:T(8,128)(2,1)S(1)}, u32[]{:S(2)}) copy-start(bf16[1024,12,64]{0,2,1:T(8,128)(2,1)S(1)} %get-tuple-element.1432) | copy-start | bytes 4718596 | tf_op jit(solution)/shard_map/while
  612.3 10.1 copy-start.5
  612.3 10.1 copy-start.24
  626.6 7.7 slice-start.8
  634.3 7.6 copy-start.17
  656.3 8.0 slice-start
  751.9 13.3 slice-start.6
  756.3 8.9 slice-start.7
  765.2 7.9 copy-start.36
  765.2 10.8 copy-start.49
  765.2 10.8 copy-start.55
  765.2 10.8 copy-start.59
  765.2 10.7 copy-start.62
  776.2 11.1 copy-start.9
  789.7 12.6 copy-start.4
  806.0 76.4 %copy-start.15 = (bf16[1024,12,64]{0,2,1:T(8,128)(2,1)}, bf16[1024,12,64]{0,2,1:T(8,128)(2,1)S(1)}, u32[]{:S(2)}) copy-start(bf16[1024,12,64]{0,2,1:T(8,128)(2,1)S(1)} %get-tuple-element.1432) | copy-start | bytes 4718596 | tf_op jit(solution)/shard_map/while
  827.6 10.1 copy-start.5
  827.6 10.1 copy-start.24
  841.8 9.6 slice-start.8
  851.4 10.1 copy-start.17
  875.8 8.0 slice-start
  972.8 13.3 slice-start.6
  977.1 8.9 slice-start.7
  986.0 7.9 copy-start.36
  986.1 10.8 copy-start.49
  986.1 10.8 copy-start.55
  986.1 10.8 copy-start.59
  986.1 10.7 copy-start.62
  1002.7 280.6 %reduce-scatter.5.cloned.1.call-start = ((), (), s32[]{:S(2)}) async-start(), calls=%async_computation.12 | async-start | bytes 7299072 | tf_op jit(solution)/shard_map/reduce_scatter | solution.py:353
  1003.3 421.8 %reduce-scatter.9.cloned.1.call-start = ((), (), s32[]{:S(2)}) async-start(), calls=%async_computation.14 | async-start | bytes 9732096 | tf_op jit(solution)/shard_map/reduce_scatter | solution.py:353
  1004.0 563.0 %reduce-scatter.11.cloned.1.call-start = ((), (), s32[]{:S(2)}) async-start(), calls=%async_computation.15 | async-start | bytes 9732096 | tf_op jit(solution)/shard_map/reduce_scatter | solution.py:353
  1010.9 81.4 %all-to-all-start.3 = ((bf16[2,1024,768]{2,0,1:T(2,128)(2,1)}), bf16[2,1024,768]{2,0,1:T(2,128)(2,1)S(1)}, u32[]{:S(2)}, u32[]{:S(2)}) async-start(bf16[2,1024,768]{2,0,1:T(2,128)(2,1)} %copy.119), calls=%async_computation.3 | async-start | bytes 6291456 | tf_op jit(solution)/shard_map/all_to_all | solution.py:356
  1023.4 73.6 %copy-start.93 = (s32[1,8]{1,0:T(1,128)S(1)}, s32[1,8]{1,0:T(1,128)}, u32[]{:S(2)}) copy-start(s32[1,8]{1,0:T(1,128)} %param.21) | copy-start | bytes 100
  1023.4 74.3 %copy-start.65 = (f32[768]{0:T(1024)S(1)}, f32[768]{0:T(1024)}, u32[]{:S(2)}) copy-start(f32[768]{0:T(1024)} %get-tuple-element.639) | copy-start | bytes 9220
  1023.4 74.3 %copy-start.68 = (f32[768]{0:T(1024)S(1)}, f32[768]{0:T(1024)}, u32[]{:S(2)}) copy-start(f32[768]{0:T(1024)} %get-tuple-element.636) | copy-start | bytes 9220
  1023.4 74.3 %copy-start.71 = (f32[768]{0:T(1024)S(1)}, f32[768]{0:T(1024)}, u32[]{:S(2)}) copy-start(f32[768]{0:T(1024)} %get-tuple-element.635) | copy-start | bytes 9220
  1092.3 102.2 %all-to-all-start.1 = ((bf16[2,1024,768]{2,0,1:T(2,128)(2,1)}), bf16[2,1024,768]{2,0,1:T(2,128)(2,1)}, u32[]{:S(2)}, u32[]{:S(2)}) async-start(bf16[2,1024,768]{2,0,1:T(2,128)(2,1)} %copy.110), calls=%async_computation.1 | async-start | bytes 6291456 | tf_op jit(solution)/shard_map/all_to_all | solution.py:355
  1205.7 361.3 %copy-start.1 = (bf16[8,256,768]{2,1,0:T(8,128)(2,1)S(1)}, bf16[8,256,768]{2,1,0:T(8,128)(2,1)}, u32[]{:S(2)}) copy-start(bf16[8,256,768]{2,1,0:T(8,128)(2,1)} %param.19) | copy-start | bytes 9437188
  (141 other events, 490.9 us)
Sparse Core Ops, SparseCore 0:
  10.8 96.0 all-gather.6
  109.7 88.6 all-gather.4
  201.2 63.2 all-gather.8
  267.2 61.8 all-gather.10
  1002.8 153.7 reduce-scatter.6
  1162.8 120.4 reduce-scatter.4
  1289.8 135.2 reduce-scatter.8
  1431.6 135.3 reduce-scatter.10
